TPU v7x, 512 devices: a whole 4x8x8 slice. The times are simulated.
512 devices in a mesh: dp: 16 (over y, core), table: 32 (over x, z).
Axes of the slice: x: 4, y: 8, z: 8, core: 2. Of those that a mesh axis runs over, the one named last changes fastest.
Arguments:
- embedded: bfloat16 [2, 32768, 4096], P(None, 'dp', 'table'), may hold values from -1.1953125 to 1.1953125
- resid_grad: bfloat16 [2, 32768, 4096], P(None, 'dp', 'table'), may hold values from -0.29882812 to 0.29882812
- query_grad: bfloat16 [2, 32768, 2048], P(None, ('dp', 'table')), may hold values from -0.59765625 to 0.59765625
- query_weight: bfloat16 [4096, 2048], P('table'), may hold values from -0.09375 to 0.09375
- ngram_rows: int32 [2, 32768, 4], P(None, 'dp'), may hold values from 0 to 3199999, as said below
- touched_rows: int32 [32, 4, 12], replicated, may hold values from -1 to 3199999, as said below
- row_values: float32 [32, 4, 12, 1024], P('table'), may hold values from -6 to 6
- row_mean: float32 [32, 4, 12, 1024], P('table'), may hold values from -0.6 to 0.6
- row_square: float32 [32, 4, 12, 1024], P('table'), may hold values from 0.01 to 0.1
Outputs:
- weight_grad: float32 [4096, 2048], P('table')
- new_values: float32 [32, 4, 12, 1024], P('table')
- new_mean: float32 [32, 4, 12, 1024], P('table')
- new_square: float32 [32, 4, 12, 1024], P('table')
Inputs may be any that keep to these rules, and one draw needn't show every extreme that they name: `touched_rows`: owner o's list for slice s holds 1 to 12 distinct row ids of [o * 100000, (o + 1) * 100000) first, then -1; in every slice some owner's list is full. `ngram_rows`: every id of slice s is one of the listed rows of owner id // 100000 for slice s.
All inputs are finite; a program needn't handle non-finite values.
Results may differ from a plain program's by a relative error of at most 0.0003.
Values may be sent and summed in bfloat16 or wider, within the bound.
No kernel may reach another device: no remote copies, remote signals or barrier semaphores. Data moves between devices by JAX's collectives and lax.ppermute only.
A program may use at most 64 MiB of HBM per device.

v0:
```python
import jax
import jax.numpy as jnp
from jax import lax
from jax.sharding import Mesh, PartitionSpec as P

SW = 1024
beta_one = 0.9
beta_two = 0.95
learn_rate = 0.01
adam_eps = 1e-08
adam_step = 10
f32 = jnp.float32
bf16 = jnp.bfloat16


def adam_rows(grads, values, mean, square, live):
    corr_one = 1.0 - beta_one**adam_step
    corr_two = 1.0 - beta_two**adam_step
    mean_next = beta_one * mean + (1.0 - beta_one) * grads
    square_next = beta_two * square + (1.0 - beta_two) * grads * grads
    update = learn_rate * (mean_next / corr_one) / (jnp.sqrt(square_next / corr_two) + adam_eps)
    values_next = values - update
    return (
        jnp.where(live, values_next, values),
        jnp.where(live, mean_next, mean),
        jnp.where(live, square_next, square),
    )


def over_tokens(left, right):
    return lax.dot_general(left, right, (((0,), (0,)), ((), ())), preferred_element_type=f32)


def shift(array, axis, step):
    size = lax.axis_size(axis)
    return lax.ppermute(array, axis, [(i, (i + step) % size) for i in range(size)])


def local(
    embedded,
    resid_grad,
    query_grad,
    query_weight,
    ngram_rows,
    touched_rows,
    row_values,
    row_mean,
    row_square,
):
    micro, group, width = embedded.shape
    per, hidden = query_grad.shape[1:]
    nx, nz, ny = (lax.axis_size("x"), lax.axis_size("z"), lax.axis_size("y"))
    x_idx, z_idx, core = (lax.axis_index("x"), lax.axis_index("z"), lax.axis_index("core"))
    tables, slices, entries = touched_rows.shape
    part = hidden // nx
    tokens = micro * group
    groups = ny * 2
    rows_p = width // groups

    def token_order(array):
        tail = array.shape[2:]
        array = array.reshape((micro, nx, nz, per) + tail)
        return array.transpose((2, 1, 0, 3) + tuple(range(4, array.ndim))).reshape((tokens,) + tail)

    def by_part(array):
        return array.reshape(-1, nx, part).transpose(1, 0, 2)

    query = lax.all_to_all(by_part(query_grad), "x", 0, 0, tiled=True)
    query = lax.all_gather(query.reshape(nx * micro * per, part), "z", axis=0, tiled=True)
    weight = lax.all_to_all(by_part(query_weight), "x", 0, 0, tiled=True)
    emb = token_order(embedded)
    half = tokens // 2
    emb_back = shift(emb, "x", 1)
    emb_front = shift(emb, "x", -1)
    far_low = shift(emb_back[:half], "x", 1)
    far_high = shift(emb_front[half:], "x", -1)
    emb_far = jnp.concatenate([far_low, far_high], axis=0)
    emb_all = [emb, emb_front, emb_far, emb_back]
    ids = token_order(ngram_rows)
    lists = touched_rows.transpose(1, 2, 0).reshape(slices, entries * tables)

    def onehot(ids_of, list_of):
        return (ids_of[:, None] == list_of[None, :]).astype(bf16)

    own_ids = lax.dynamic_index_in_dim(ids, x_idx, 1, False)
    own_list = lax.dynamic_index_in_dim(lists, x_idx, 0, False)
    resid_rows = over_tokens(onehot(own_ids, own_list), token_order(resid_grad))
    row_parts = []
    for s in range(slices):
        seg = over_tokens(onehot(ids[:, s], lists[s]), query)
        high = lax.reduce_precision(seg, 8, 7)
        low = (seg - high).astype(bf16)
        one = lax.dot_general(
            high.astype(bf16), weight[s], (((1,), (1,)), ((), ())), preferred_element_type=f32
        )
        two = lax.dot_general(low, weight[s], (((1,), (1,)), ((), ())), preferred_element_type=f32)
        row_parts.append(one + two + jnp.where(x_idx == s, resid_rows, 0.0))
    row_sum = jnp.stack(row_parts).reshape(groups, slices * entries // groups * tables, width)
    w_parts = [over_tokens(piece, query) for piece in emb_all]
    w_sum = jnp.stack(w_parts)
    lanes = 128
    w_sum = w_sum.reshape(nx, groups, rows_p, part // lanes, lanes).transpose(1, 0, 3, 2, 4)
    w_sum = w_sum.reshape(groups, nx * part // lanes * rows_p, lanes)
    both = jnp.concatenate([w_sum, row_sum], axis=1)
    both = both.reshape(ny, 2, both.shape[1], lanes)
    first = core == 0
    send = jnp.where(first, both[:, 1], both[:, 0])
    keep = jnp.where(first, both[:, 0], both[:, 1])
    pair = keep + shift(send, "core", 1)
    pieces = lax.all_to_all(pair, "y", 0, 0, tiled=True)
    total = jnp.sum(pieces, axis=0)
    w_rows = nx * part // lanes * rows_p
    w_mine = total[:w_rows].reshape(nx, part // lanes * rows_p, lanes)
    twice = jnp.concatenate([w_mine, w_mine], axis=0)
    w_mine = lax.dynamic_slice_in_dim(twice, nx - x_idx, nx, 0)
    w_mine = lax.all_to_all(w_mine, "x", 0, 0, tiled=True).reshape(w_rows, lanes)
    pairs = slices * entries // groups
    r_mine = total[w_rows:].reshape(pairs, tables, width).transpose(1, 0, 2)
    r_mine = lax.all_to_all(r_mine, ("x", "z"), 0, 0, tiled=True)
    r_mine = jnp.sum(r_mine.reshape(nx, nz, pairs, width), axis=0)
    r_mine = r_mine.transpose(1, 0, 2).reshape(pairs * nz, lanes)
    piece = jnp.concatenate([w_mine, r_mine], axis=0)
    spread = jnp.broadcast_to(piece[None], (ny,) + piece.shape)
    mine = lax.all_to_all(spread, "y", 0, 0, tiled=True)
    other = shift(mine, "core", 1)
    full = jnp.stack([jnp.where(first, mine, other), jnp.where(first, other, mine)], axis=1)
    full = full.reshape((groups,) + piece.shape)
    weight_grad = full[:, :w_rows].reshape(groups, hidden // lanes, rows_p, lanes)
    weight_grad = weight_grad.transpose(0, 2, 1, 3).reshape(width, hidden)
    grads = full[:, w_rows:].reshape(slices, entries, nz * width)
    mine_rows = lax.dynamic_index_in_dim(touched_rows, x_idx * nz + z_idx, 0, False)
    live = (mine_rows >= 0)[..., None]
    values_next, mean_next, square_next = adam_rows(
        grads, row_values[0], row_mean[0], row_square[0], live
    )
    return (weight_grad, values_next[None], mean_next[None], square_next[None])


def solution(mesh):
    fine = Mesh(mesh.devices.reshape(8, 2, 4, 8), ("y", "core", "x", "z"))
    dp, table = (("y", "core"), ("x", "z"))
    placed = (
        P(None, dp, table),
        P(None, dp, table),
        P(None, dp + table, None),
        P(table, None),
        P(None, dp, None),
        P(),
        P(table, None, None, None),
        P(table, None, None, None),
        P(table, None, None, None),
    )
    return jax.shard_map(
        local,
        mesh=fine,
        in_specs=placed,
        out_specs=(
            P(table, None),
            P(table, None, None, None),
            P(table, None, None, None),
            P(table, None, None, None),
        ),
        check_vma=False,
    )
```

profile of v0, /device:TPU:1, one launch (start us, length us, event | category | flops | bytes accessed | tf_op | source)
XLA Modules:
  0.0 213.3 jit_solution(14318160484905589885)
XLA Ops:
  7.2 1.5 reshape.141
  8.9 11.7 %all_to_all.30 = bf16[4,128,512]{2,1,0:T(8,128)(2,1)S(1)} all-to-all(bf16[4,128,512]{2,1,0:T(8,128)(2,1)S(1)} %copy.185), channel_id=1, replica_groups=mesh['y'=8,'core'=2,'x'=4,'z'=8] {'x'}, dimensions={0} | all-to-all | bytes 1048576 | tf_op jit(solution)/shard_map/all_to_all | solution.py:68
  21.7 2.2 %collective-permute-start.1 = (bf16[4096,128]{1,0:T(8,128)(2,1)S(1)}, bf16[4096,128]{1,0:T(8,128)(2,1)}, u32[]{:S(2)}, u32[]{:S(2)}) collective-permute-start(bf16[4096,128]{1,0:T(8,128)(2,1)S(1)} %bitcast.145), channel_id=1, source_target_pairs={{0,8},{8,16},{16,24},{24,0},{1,9},{9,17},{17,25},{25,1},{2,10},{10... | collective-permute-start | bytes 3145736 | tf_op jit(solution)/shard_map/ppermute | solution.py:36
  23.9 4.3 %collective-permute-start = (bf16[4096,128]{1,0:T(8,128)(2,1)S(1)}, bf16[4096,128]{1,0:T(8,128)(2,1)}, u32[]{:S(2)}, u32[]{:S(2)}) collective-permute-start(bf16[4096,128]{1,0:T(8,128)(2,1)S(1)} %bitcast.146), channel_id=1, source_target_pairs={{0,24},{8,0},{16,8},{24,16},{1,25},{9,1},{17,9},{25,17},{2,26},{10... | collective-permute-start | bytes 3145736 | tf_op jit(solution)/shard_map/ppermute | solution.py:36
  28.3 2.0 copy.189
  30.3 3.5 %all-to-all-start.1 = ((bf16[4,128,512]{1,2,0:T(8,128)(2,1)}), bf16[4,128,512]{1,2,0:T(8,128)(2,1)S(1)}, u32[]{:S(2)}, u32[]{:S(2)}) async-start(bf16[4,128,512]{1,2,0:T(8,128)(2,1)} %bitcast.22), calls=%async_computation.1 | async-start | bytes 1048576 | tf_op jit(solution)/shard_map/all_to_all | solution.py:70
  35.7 1.3 copy.184
  37.1 3.7 %fusion = f32[384,128]{1,0:T(8,128)S(1)} fusion(bf16[4096,128]{1,0:T(8,128)(2,1)} %bitcast.152, s32[384]{0:T(512)S(1)} %dynamic-slice_reduce_fusion, s32[4096]{0:T(1024)S(1)} %bitcast.166), kind=kOutput, calls=%fused_computation.3 | convolution fusion | flops 404226048 | bytes 1263104 | tf_op jit(solution)/shard_map/dot_general | solution.py:31
  40.8 3.9 %collective-permute-done = bf16[4096,128]{1,0:T(8,128)(2,1)} collective-permute-done((bf16[4096,128]{1,0:T(8,128)(2,1)S(1)}, bf16[4096,128]{1,0:T(8,128)(2,1)}, u32[]{:S(2)}, u32[]{:S(2)}) %collective-permute-start) | collective-permute-done | bytes 1048608 | tf_op jit(solution)/shard_map/ppermute | solution.py:36
  45.8 5.4 %collective-permute-start.3 = (bf16[2048,128]{1,0:T(8,128)(2,1)S(1)}, bf16[2048,128]{1,0:T(8,128)(2,1)}, u32[]{:S(2)}, u32[]{:S(2)}) collective-permute-start(bf16[2048,128]{1,0:T(8,128)(2,1)S(1)} %slice.91), channel_id=1, source_target_pairs={{0,24},{8,0},{16,8},{24,16},{1,25},{9,1},{17,9},{25,17},{2,26},{10... | collective-permute-start | bytes 1572872 | tf_op jit(solution)/shard_map/ppermute | solution.py:36
  52.3 2.1 collective-permute-start.2
  54.4 31.0 %all-gather.2.cloned.1.call-done = bf16[4096,512]{0,1:T(8,128)(2,1)} async-done(((bf16[512,512]{0,1:T(8,128)(2,1)}), bf16[4096,512]{0,1:T(8,128)(2,1)}) %all-gather.2.cloned.1.call-update) | async-done | bytes 4194320 | tf_op jit(solution)/shard_map/all_gather | solution.py:69
  85.5 4.1 %convolution_bitcast_fusion.3 = f32[1,16,8,4,128]{4,2,3,1,0:T(8,128)S(1)} fusion(bf16[4,128,4096,1]{2,1,0,3:T(8,128)(2,1)} %bitcast.138, bf16[128,4096]{1,0:T(8,128)(2,1)} %copy.184), kind=kOutput, calls=%fused_computation.26 | convolution fusion | flops 536870912 | bytes 5505024 | tf_op jit(solution)/shard_map/dot_general | solution.py:31
  89.6 2.7 %convolution_bitcast_fusion = f32[1,16,8,4,128]{4,2,3,1,0:T(8,128)S(1)} fusion(bf16[4096,128]{1,0:T(8,128)(2,1)} %collective-permute-done.1, bf16[4096,512]{0,1:T(8,128)(2,1)S(1)} %copy-done), kind=kOutput, calls=%fused_computation.23 | convolution fusion | flops 536870912 | bytes 5505024 | tf_op jit(solution)/shard_map/dot_general | solution.py:31
  92.4 2.7 %convolution_bitcast_fusion.2 = f32[1,16,8,4,128]{4,2,3,1,0:T(8,128)S(1)} fusion(bf16[4096,128]{1,0:T(8,128)(2,1)} %collective-permute-done, bf16[4096,512]{0,1:T(8,128)(2,1)S(1)} %copy-done), kind=kOutput, calls=%fused_computation.25 | convolution fusion | flops 536870912 | bytes 5505024 | tf_op jit(solution)/shard_map/dot_general | solution.py:31
  95.1 2.6 %convolution_bitcast_fusion.1 = f32[1,16,8,4,128]{4,2,3,1,0:T(8,128)S(1)} fusion(bf16[4096,512]{0,1:T(8,128)(2,1)S(1)} %copy-done, bf16[2048,128]{1,0:T(8,128)(2,1)} %collective-permute-done.3, bf16[2048,128]{1,0:T(8,128)(2,1)S(1)} %collective-permute-done.2), kind=kOutput, calls=%fused_computation.24 | convolution fusion | flops 538968064 | bytes 5505024 | tf_op jit(solution)/shard_map/dot_general | solution.py:31
  97.9 2.5 %fusion.5 = f32[384,512]{1,0:T(8,128)S(1)} fusion(bf16[4096,512]{0,1:T(8,128)(2,1)S(1)} %copy-done, s32[384]{0:T(512)S(1)} %eq.126, s32[4096]{0:T(1024)S(1)} %bitcast.165), kind=kOutput, calls=%fused_computation.9 | convolution fusion | flops 1613758464 | bytes 4998656 | tf_op jit(solution)/shard_map/dot_general | solution.py:31
  100.6 4.8 %fusion.4 = f32[384,512]{1,0:T(8,128)S(1)} fusion(bf16[4096,512]{0,1:T(8,128)(2,1)} %all-gather.2.cloned.1.call-done, s32[384]{0:T(512)S(1)} %eq.120, s32[4096]{0:T(1024)S(1)} %bitcast.164), kind=kOutput, calls=%fused_computation.8 | convolution fusion | flops 1613758464 | bytes 4998656 | tf_op jit(solution)/shard_map/dot_general | solution.py:31
  105.7 2.5 %fusion.3 = f32[384,512]{1,0:T(8,128)S(1)} fusion(bf16[4096,512]{0,1:T(8,128)(2,1)S(1)} %copy-done.1, s32[384]{0:T(512)S(1)} %eq.114, s32[4096]{0:T(1024)S(1)} %bitcast.163), kind=kOutput, calls=%fused_computation.7 | convolution fusion | flops 1613758464 | bytes 4998656 | tf_op jit(solution)/shard_map/dot_general | solution.py:31
  108.5 2.7 %fusion.2 = f32[384,512]{1,0:T(8,128)S(1)} fusion(bf16[4096,512]{0,1:T(8,128)(2,1)S(1)} %copy-done.1, s32[384]{0:T(512)S(1)} %eq.103, s32[4096]{0:T(1024)S(1)} %bitcast.162), kind=kOutput, calls=%fused_computation.6 | convolution fusion | flops 1613758464 | bytes 4998656 | tf_op jit(solution)/shard_map/dot_general | solution.py:31
  112.8 2.7 %collective-permute-start.4 = (f32[8,224,128]{2,1,0:T(8,128)S(1)}, f32[8,224,128]{2,1,0:T(8,128)S(1)}, u32[]{:S(2)}, u32[]{:S(2)}) collective-permute-start(f32[8,224,128]{2,1,0:T(8,128)S(1)} %select_bitcast_fusion), channel_id=1, source_target_pairs={{0,32},{32,0},{1,33},{33,1},{2,34},{34,2},{3,35},{35,3},{4,36},{36... | collective-permute-start | bytes 2752520 | tf_op jit(solution)/shard_map/ppermute | solution.py:36
  115.5 2.1 collective-permute-done.4
  117.6 1.1 fusion.30
  118.7 6.5 %all-to-all-start.2 = ((f32[8,224,128]{2,1,0:T(8,128)}), f32[8,224,128]{2,1,0:T(8,128)S(1)}, u32[]{:S(2)}, u32[]{:S(2)}) async-start(f32[8,224,128]{2,1,0:T(8,128)} %fusion.30), calls=%async_computation.2 | async-start | bytes 1835008 | tf_op jit(solution)/shard_map/all_to_all | solution.py:110
  125.2 26.4 %all-to-all-done.2 = f32[8,224,128]{2,1,0:T(8,128)S(1)} async-done(((f32[8,224,128]{2,1,0:T(8,128)}), f32[8,224,128]{2,1,0:T(8,128)S(1)}, u32[]{:S(2)}, u32[]{:S(2)}) %all-to-all-start.2) | async-done | bytes 917536 | tf_op jit(solution)/shard_map/all_to_all | solution.py:110
  152.3 6.6 %all-to-all-start.4 = ((f32[32,3,128]{2,1,0:T(4,128)}), f32[32,3,128]{2,1,0:T(4,128)S(1)}, u32[]{:S(2)}, u32[]{:S(2)}) async-start(f32[32,3,128]{2,1,0:T(4,128)} %copy.200), calls=%async_computation.4 | async-start | bytes 131072 | tf_op jit(solution)/shard_map/all_to_all | solution.py:119
  159.6 8.2 %all-to-all-done.4 = f32[32,3,128]{2,1,0:T(4,128)S(1)} async-done(((f32[32,3,128]{2,1,0:T(4,128)}), f32[32,3,128]{2,1,0:T(4,128)S(1)}, u32[]{:S(2)}, u32[]{:S(2)}) %all-to-all-start.4) | async-done | bytes 49184 | tf_op jit(solution)/shard_map/all_to_all | solution.py:119
  167.8 3.3 %all-to-all-start.3 = ((f32[4,32,128]{2,1,0:T(8,128)}), f32[4,32,128]{2,1,0:T(8,128)S(1)}, u32[]{:S(2)}, u32[]{:S(2)}) async-start(f32[4,32,128]{2,1,0:T(8,128)} %fusion.45), calls=%async_computation.3 | async-start | bytes 131072 | tf_op jit(solution)/shard_map/all_to_all | solution.py:116
  171.1 4.4 %all-to-all-done.3 = f32[4,32,128]{2,1,0:T(8,128)S(1)} async-done(((f32[4,32,128]{2,1,0:T(8,128)}), f32[4,32,128]{2,1,0:T(8,128)S(1)}, u32[]{:S(2)}, u32[]{:S(2)}) %all-to-all-start.3) | async-done | bytes 65568 | tf_op jit(solution)/shard_map/all_to_all | solution.py:116
  175.6 18.7 %all_to_all.31 = f32[8,152,128]{2,1,0:T(8,128)S(1)} all-to-all(f32[8,152,128]{2,1,0:T(8,128)S(1)} %broadcast_in_dim.34), channel_id=1, replica_groups=mesh['y'=8,'core'=2,'x'=4,'z'=8] {'y'}, dimensions={0} | all-to-all | bytes 1245184 | tf_op jit(solution)/shard_map/all_to_all | solution.py:124
  194.3 6.2 %collective-permute-start.5 = (f32[8,152,128]{2,1,0:T(8,128)S(1)}, f32[8,152,128]{2,1,0:T(8,128)S(1)}, u32[]{:S(2)}, u32[]{:S(2)}) collective-permute-start(f32[8,152,128]{2,1,0:T(8,128)S(1)} %all_to_all.31), channel_id=1, source_target_pairs={{0,32},{32,0},{1,33},{33,1},{2,34},{34,2},{3,35},{35,3},{4,36},{36... | collective-permute-start | bytes 1867784 | tf_op jit(solution)/shard_map/ppermute | solution.py:36
  200.8 1.4 collective-permute-done.5
  (75 shorter events, 13.8 us)
Async XLA Ops:
  7.2 14.5 %copy-start.2 = (bf16[2,2048,128]{2,1,0:T(8,128)(2,1)S(1)}, bf16[2,2048,128]{2,1,0:T(8,128)(2,1)}, u32[]{:S(2)}) copy-start(bf16[2,2048,128]{2,1,0:T(8,128)(2,1)} %param.9) | copy-start | bytes 3145732
  7.2 78.3 %all-gather.2.cloned.1.call-start = ((), (), s32[]{:S(2)}) async-start(), calls=%async_computation.6 | async-start | bytes 4718592 | tf_op jit(solution)/shard_map/all_gather | solution.py:69
  8.7 25.1 %copy-start.4 = (s32[32,4,12]{0,1,2:T(4,128)S(1)}, s32[32,4,12]{0,1,2:T(4,128)}, u32[]{:S(2)}) copy-start(s32[32,4,12]{0,1,2:T(4,128)} %param.14) | copy-start | bytes 18436
  8.7 25.2 %copy-start.8 = (s32[2,2048,4]{1,2,0:T(4,128)S(1)}, s32[2,2048,4]{1,2,0:T(4,128)}, u32[]{:S(2)}) copy-start(s32[2,2048,4]{1,2,0:T(4,128)} %param.13) | copy-start | bytes 196612
  8.8 25.6 %copy-start.3 = (bf16[2,2048,128]{2,1,0:T(8,128)(2,1)S(1)}, bf16[2,2048,128]{2,1,0:T(8,128)(2,1)}, u32[]{:S(2)}) copy-start(bf16[2,2048,128]{2,1,0:T(8,128)(2,1)} %param.10) | copy-start | bytes 3145732
  21.7 29.5 %collective-permute-start.1 = (bf16[4096,128]{1,0:T(8,128)(2,1)S(1)}, bf16[4096,128]{1,0:T(8,128)(2,1)}, u32[]{:S(2)}, u32[]{:S(2)}) collective-permute-start(bf16[4096,128]{1,0:T(8,128)(2,1)S(1)} %bitcast.145), channel_id=1, source_target_pairs={{0,8},{8,16},{16,24},{24,0},{1,9},{9,17},{17,25},{25,1},{2,10},{10... | collective-permute-start | bytes 3145736 | tf_op jit(solution)/shard_map/ppermute | solution.py:36
  23.9 20.8 %collective-permute-start = (bf16[4096,128]{1,0:T(8,128)(2,1)S(1)}, bf16[4096,128]{1,0:T(8,128)(2,1)}, u32[]{:S(2)}, u32[]{:S(2)}) collective-permute-start(bf16[4096,128]{1,0:T(8,128)(2,1)S(1)} %bitcast.146), channel_id=1, source_target_pairs={{0,24},{8,0},{16,8},{24,16},{1,25},{9,1},{17,9},{25,17},{2,26},{10... | collective-permute-start | bytes 3145736 | tf_op jit(solution)/shard_map/ppermute | solution.py:36
  30.3 70.1 %all-to-all-start.1 = ((bf16[4,128,512]{1,2,0:T(8,128)(2,1)}), bf16[4,128,512]{1,2,0:T(8,128)(2,1)S(1)}, u32[]{:S(2)}, u32[]{:S(2)}) async-start(bf16[4,128,512]{1,2,0:T(8,128)(2,1)} %bitcast.22), calls=%async_computation.1 | async-start | bytes 1048576 | tf_op jit(solution)/shard_map/all_to_all | solution.py:70
  45.8 49.3 %collective-permute-start.3 = (bf16[2048,128]{1,0:T(8,128)(2,1)S(1)}, bf16[2048,128]{1,0:T(8,128)(2,1)}, u32[]{:S(2)}, u32[]{:S(2)}) collective-permute-start(bf16[2048,128]{1,0:T(8,128)(2,1)S(1)} %slice.91), channel_id=1, source_target_pairs={{0,24},{8,0},{16,8},{24,16},{1,25},{9,1},{17,9},{25,17},{2,26},{10... | collective-permute-start | bytes 1572872 | tf_op jit(solution)/shard_map/ppermute | solution.py:36
  52.3 42.8 %collective-permute-start.2 = (bf16[2048,128]{1,0:T(8,128)(2,1)S(1)}, bf16[2048,128]{1,0:T(8,128)(2,1)S(1)}, u32[]{:S(2)}, u32[]{:S(2)}) collective-permute-start(bf16[2048,128]{1,0:T(8,128)(2,1)S(1)} %slice.90), channel_id=1, source_target_pairs={{0,8},{8,16},{16,24},{24,0},{1,9},{9,17},{17,25},{25,1},{2,10},{10... | collective-permute-start | bytes 1572872 | tf_op jit(solution)/shard_map/ppermute | solution.py:36
  85.5 4.2 %copy-start = (bf16[4096,512]{0,1:T(8,128)(2,1)S(1)}, bf16[4096,512]{0,1:T(8,128)(2,1)}, u32[]{:S(2)}) copy-start(bf16[4096,512]{0,1:T(8,128)(2,1)} %all-gather.2.cloned.1.call-done) | copy-start | bytes 12582916
  100.6 5.1 %copy-start.1 = (bf16[4096,512]{0,1:T(8,128)(2,1)S(1)}, bf16[4096,512]{0,1:T(8,128)(2,1)}, u32[]{:S(2)}) copy-start(bf16[4096,512]{0,1:T(8,128)(2,1)} %all-gather.2.cloned.1.call-done) | copy-start | bytes 12582916
  112.8 4.8 %collective-permute-start.4 = (f32[8,224,128]{2,1,0:T(8,128)S(1)}, f32[8,224,128]{2,1,0:T(8,128)S(1)}, u32[]{:S(2)}, u32[]{:S(2)}) collective-permute-start(f32[8,224,128]{2,1,0:T(8,128)S(1)} %select_bitcast_fusion), channel_id=1, source_target_pairs={{0,32},{32,0},{1,33},{33,1},{2,34},{34,2},{3,35},{35,3},{4,36},{36... | collective-permute-start | bytes 2752520 | tf_op jit(solution)/shard_map/ppermute | solution.py:36
  118.7 32.9 %all-to-all-start.2 = ((f32[8,224,128]{2,1,0:T(8,128)}), f32[8,224,128]{2,1,0:T(8,128)S(1)}, u32[]{:S(2)}, u32[]{:S(2)}) async-start(f32[8,224,128]{2,1,0:T(8,128)} %fusion.30), calls=%async_computation.2 | async-start | bytes 1835008 | tf_op jit(solution)/shard_map/all_to_all | solution.py:110
  152.3 15.5 %all-to-all-start.4 = ((f32[32,3,128]{2,1,0:T(4,128)}), f32[32,3,128]{2,1,0:T(4,128)S(1)}, u32[]{:S(2)}, u32[]{:S(2)}) async-start(f32[32,3,128]{2,1,0:T(4,128)} %copy.200), calls=%async_computation.4 | async-start | bytes 131072 | tf_op jit(solution)/shard_map/all_to_all | solution.py:119
  167.8 7.7 %all-to-all-start.3 = ((f32[4,32,128]{2,1,0:T(8,128)}), f32[4,32,128]{2,1,0:T(8,128)S(1)}, u32[]{:S(2)}, u32[]{:S(2)}) async-start(f32[4,32,128]{2,1,0:T(8,128)} %fusion.45), calls=%async_computation.3 | async-start | bytes 131072 | tf_op jit(solution)/shard_map/all_to_all | solution.py:116
  194.3 9.2 %copy-start.5 = (f32[1,4,12,1024]{3,1,2,0:T(4,128)S(1)}, f32[1,4,12,1024]{3,1,2,0:T(4,128)}, u32[]{:S(2)}) copy-start(f32[1,4,12,1024]{3,1,2,0:T(4,128)} %param.17) | copy-start | bytes 589828
  194.3 9.2 %copy-start.6 = (f32[1,4,12,1024]{3,1,2,0:T(4,128)S(1)}, f32[1,4,12,1024]{3,1,2,0:T(4,128)}, u32[]{:S(2)}) copy-start(f32[1,4,12,1024]{3,1,2,0:T(4,128)} %param.16) | copy-start | bytes 589828
  194.3 9.2 %copy-start.7 = (f32[1,4,12,1024]{3,1,2,0:T(4,128)S(1)}, f32[1,4,12,1024]{3,1,2,0:T(4,128)}, u32[]{:S(2)}) copy-start(f32[1,4,12,1024]{3,1,2,0:T(4,128)} %param.15) | copy-start | bytes 589828
  194.3 7.9 %collective-permute-start.5 = (f32[8,152,128]{2,1,0:T(8,128)S(1)}, f32[8,152,128]{2,1,0:T(8,128)S(1)}, u32[]{:S(2)}, u32[]{:S(2)}) collective-permute-start(f32[8,152,128]{2,1,0:T(8,128)S(1)} %all_to_all.31), channel_id=1, source_target_pairs={{0,32},{32,0},{1,33},{33,1},{2,34},{34,2},{3,35},{35,3},{4,36},{36... | collective-permute-start | bytes 1867784 | tf_op jit(solution)/shard_map/ppermute | solution.py:36
Sparse Core Ops, SparseCore 0:
  21.8 63.6 all-gather.1
where the time goes:
time: 214 us; the launch traced here: 213 us
  waiting for transfers between devices  77.4 us (36%)
  starting transfers between devices  42.9 us (20%)
  blocking collectives  30.4 us (14%)
  matrix products  30.4 us (14%)
  local copies, waits for them, and re-layouts  14.8 us (7%)
  between operations  14.5 us (7%)
  other arithmetic  2.73 us (1%)
    all_gather x1, waiting for transfers between devices, local(): lax.all_gather(query.reshape(nx * micro * per, part), 'z', axis=0, tiled=...  31 us
    dot_general x9, matrix products, over_tokens(): lax.dot_general(left, right, (((0,), (0,)), ((), ())), preferred_element_...  28.3 us
    all_to_all x1, waiting for transfers between devices, local(): pieces = lax.all_to_all(pair, 'y', 0, 0, tiled=True)  26.4 us
    ppermute x6, starting transfers between devices, shift(): lax.ppermute(array, axis, [(i, (i + step) % size) for i in range(size)])  23 us
    all_to_all x1, blocking collectives, local(): mine = lax.all_to_all(spread, 'y', 0, 0, tiled=True)  18.7 us
    all_to_all x1, blocking collectives, local(): query = lax.all_to_all(by_part(query_grad), 'x', 0, 0, tiled=True)  11.7 us
    all_to_all x1, waiting for transfers between devices, local(): r_mine = lax.all_to_all(r_mine, ('x', 'z'), 0, 0, tiled=True)  8.21 us
    ppermute x6, waiting for transfers between devices, shift(): lax.ppermute(array, axis, [(i, (i + step) % size) for i in range(size)])  7.41 us
  transfers between devices with their start and end apart: 11, of which 7 were waited for; matrix products, arithmetic and copies ran while one was open for 13% of the time, Pallas kernels for 0%

commit v1 on v0

--- a/solution.py
+++ b/solution.py
@@ -66,7 +66,12 @@
         return array.reshape(-1, nx, part).transpose(1, 0, 2)
 
     query = lax.all_to_all(by_part(query_grad), "x", 0, 0, tiled=True)
-    query = lax.all_gather(query.reshape(nx * micro * per, part), "z", axis=0, tiled=True)
+    query = jnp.concatenate(
+        lax.all_to_all(
+            jnp.stack([query.reshape(nx * micro * per, part)] * lax.axis_size("z")), "z", 0, 0
+        ),
+        axis=0,
+    )
     weight = lax.all_to_all(by_part(query_weight), "x", 0, 0, tiled=True)
     emb = token_order(embedded)
     half = tokens // 2

time: 214 us -> 263 us (1.23)
  waiting for transfers between devices: 77.4 us -> 111 us
  local copies, waits for them, and re-layouts: 14.8 us -> 35.3 us
  between operations: 14.5 us -> 1.16 us
  starting transfers between devices: 42.9 us -> 50.2 us
    all_to_all x0 -> x1, waiting for transfers between devices: none -> 50 us  [local(): lax.all_to_all(jnp.stack([query.reshape(nx * micro * per, part)] * lax.ax...]
    all_gather x1 -> x0, waiting for transfers between devices: 31 us -> none  [local(): lax.all_gather(query.reshape(nx * micro * per, part), 'z', axis=0, tiled=...]
    ppermute x6, waiting for transfers between devices: 7.41 us -> 22.5 us  [shift(): lax.ppermute(array, axis, [(i, (i + step) % size) for i in range(size)])]
    all_to_all x0 -> x1, starting transfers between devices: none -> 11.9 us  [local(): lax.all_to_all(jnp.stack([query.reshape(nx * micro * per, part)] * lax.ax...]
    dot_general x1 -> x5, local copies, waits for them, and re-layouts: 1.31 us -> 11 us  [over_tokens(): lax.dot_general(left, right, (((0,), (0,)), ((), ())), preferred_element_...]
    all_to_all x0 -> x1, local copies, waits for them, and re-layouts: none -> 6.53 us  [local(): lax.all_to_all(jnp.stack([query.reshape(nx * micro * per, part)] * lax.ax...]
    dot_general x9, matrix products: 28.3 us -> 24.7 us  [over_tokens(): lax.dot_general(left, right, (((0,), (0,)), ((), ())), preferred_element_...]
    ppermute x6, starting transfers between devices: 23 us -> 19.9 us  [shift(): lax.ppermute(array, axis, [(i, (i + step) % size) for i in range(size)])]
  transfers between devices with their start and end apart: 11 -> 11, of which waited for: 7 -> 7; matrix products, arithmetic and copies ran while one was open for 13% -> 20% of each run, Pallas kernels for 0% -> 0%
where the time goes in v1:
time: 263 us; the launch traced here: 261 us
  waiting for transfers between devices  111 us (42%)
  starting transfers between devices  50.2 us (19%)
  local copies, waits for them, and re-layouts  35.3 us (13%)
  blocking collectives  30.3 us (12%)
  matrix products  29.2 us (11%)
  other arithmetic  3.96 us (2%)
    all_to_all x1, waiting for transfers between devices, local(): lax.all_to_all(jnp.stack([query.reshape(nx * micro * per, part)] * lax.ax...  50 us
    all_to_all x1, waiting for transfers between devices, local(): pieces = lax.all_to_all(pair, 'y', 0, 0, tiled=True)  26.4 us
    dot_general x9, matrix products, over_tokens(): lax.dot_general(left, right, (((0,), (0,)), ((), ())), preferred_element_...  24.7 us
    ppermute x6, waiting for transfers between devices, shift(): lax.ppermute(array, axis, [(i, (i + step) % size) for i in range(size)])  22.5 us
    ppermute x6, starting transfers between devices, shift(): lax.ppermute(array, axis, [(i, (i + step) % size) for i in range(size)])  19.9 us
    all_to_all x1, blocking collectives, local(): mine = lax.all_to_all(spread, 'y', 0, 0, tiled=True)  18.7 us
    all_to_all x1, starting transfers between devices, local(): lax.all_to_all(jnp.stack([query.reshape(nx * micro * per, part)] * lax.ax...  11.9 us
    all_to_all x1, blocking collectives, local(): query = lax.all_to_all(by_part(query_grad), 'x', 0, 0, tiled=True)  11.6 us
  transfers between devices with their start and end apart: 11, of which 7 were waited for; matrix products, arithmetic and copies ran while one was open for 20% of the time, Pallas kernels for 0%

profile of v1, /device:TPU:1, one launch (start us, length us, event | category | flops | bytes accessed | tf_op | source)
XLA Modules:
  0.0 261.5 jit_solution(13330926334087371776)
XLA Ops:
  2.2 11.6 %all_to_all.35 = bf16[4,128,512]{2,1,0:T(8,128)(2,1)S(1)} all-to-all(bf16[4,128,512]{2,1,0:T(8,128)(2,1)S(1)} %copy.211), channel_id=1, replica_groups=mesh['y'=8,'core'=2,'x'=4,'z'=8] {'x'}, dimensions={0} | all-to-all | bytes 1048576 | tf_op jit(solution)/shard_map/all_to_all | solution.py:68
  13.9 2.3 stack.34
  16.3 11.9 %all-to-all-start.1 = ((bf16[8,512,512]{1,2,0:T(8,128)(2,1)}), bf16[8,512,512]{1,2,0:T(8,128)(2,1)}, u32[]{:S(2)}, u32[]{:S(2)}) async-start(bf16[8,512,512]{1,2,0:T(8,128)(2,1)} %stack.34), calls=%async_computation.1 | async-start | bytes 8388608 | tf_op jit(solution)/shard_map/all_to_all | solution.py:70
  28.2 2.8 %collective-permute-start = (bf16[4096,128]{1,0:T(8,128)(2,1)S(1)}, bf16[4096,128]{1,0:T(8,128)(2,1)S(1)}, u32[]{:S(2)}, u32[]{:S(2)}) collective-permute-start(bf16[4096,128]{1,0:T(8,128)(2,1)S(1)} %bitcast.177), channel_id=1, source_target_pairs={{0,24},{8,0},{16,8},{24,16},{1,25},{9,1},{17,9},{25,17},{2,26},{10... | collective-permute-start | bytes 3145736 | tf_op jit(solution)/shard_map/ppermute | solution.py:36
  31.0 2.5 collective-permute-start.1
  33.9 18.9 %collective-permute-done = bf16[4096,128]{1,0:T(8,128)(2,1)S(1)} collective-permute-done((bf16[4096,128]{1,0:T(8,128)(2,1)S(1)}, bf16[4096,128]{1,0:T(8,128)(2,1)S(1)}, u32[]{:S(2)}, u32[]{:S(2)}) %collective-permute-start) | collective-permute-done | bytes 1048608 | tf_op jit(solution)/shard_map/ppermute | solution.py:36
  53.7 4.0 %collective-permute-start.3 = (bf16[2048,128]{1,0:T(8,128)(2,1)}, bf16[2048,128]{1,0:T(8,128)(2,1)}, u32[]{:S(2)}, u32[]{:S(2)}) collective-permute-start(bf16[2048,128]{1,0:T(8,128)(2,1)} %slice.91), channel_id=1, source_target_pairs={{0,24},{8,0},{16,8},{24,16},{1,25},{9,1},{17,9},{25,17},{2,26},{10... | collective-permute-start | bytes 1572872 | tf_op jit(solution)/shard_map/ppermute | solution.py:36
  58.6 1.9 collective-permute-start.2
  60.7 2.1 copy.220
  62.8 2.3 copy.223
  66.8 3.7 %fusion.6 = f32[384,128]{1,0:T(8,128)S(1)} fusion(bf16[4096,128]{1,0:T(8,128)(2,1)} %bitcast.186, s32[384]{0:T(512)S(1)} %dynamic-slice_reduce_fusion, s32[4096]{0:T(1024)S(1)} %bitcast.200), kind=kOutput, calls=%fused_computation.6 | convolution fusion | flops 404226048 | bytes 1263104 | tf_op jit(solution)/shard_map/dot_general | solution.py:31
  74.9 50.0 %all-to-all-done.1 = bf16[8,512,512]{1,2,0:T(8,128)(2,1)} async-done(((bf16[8,512,512]{1,2,0:T(8,128)(2,1)}), bf16[8,512,512]{1,2,0:T(8,128)(2,1)}, u32[]{:S(2)}, u32[]{:S(2)}) %all-to-all-start.1) | async-done | bytes 4194336 | tf_op jit(solution)/shard_map/all_to_all | solution.py:70
  124.9 3.5 %all-to-all-start.2 = ((bf16[4,128,512]{1,2,0:T(8,128)(2,1)}), bf16[4,128,512]{1,2,0:T(8,128)(2,1)S(1)}, u32[]{:S(2)}, u32[]{:S(2)}) async-start(bf16[4,128,512]{1,2,0:T(8,128)(2,1)} %bitcast.36), calls=%async_computation.2 | async-start | bytes 1048576 | tf_op jit(solution)/shard_map/all_to_all | solution.py:75
  128.4 6.5 %copy.213 = bf16[8,512,512]{2,1,0:T(8,128)(2,1)} copy(bf16[8,512,512]{1,2,0:T(8,128)(2,1)} %all-to-all-done.1) | data formatting | bytes 8388608 | tf_op jit(solution)/shard_map/all_to_all | solution.py:70
  134.9 6.5 %copy.214 = bf16[512,4096]{1,0:T(8,128)(2,1)} copy(bf16[512,4096]{0,1:T(8,128)(2,1)} %bitcast.162) | data formatting | bytes 8388608 | tf_op jit(solution)/shard_map/dot_general | solution.py:31
  141.5 3.8 %convolution_bitcast_fusion = f32[1,16,8,4,128]{4,2,3,1,0:T(8,128)S(1)} fusion(bf16[4,128,4096,1]{2,1,0,3:T(8,128)(2,1)} %bitcast.173, bf16[128,4096]{1,0:T(8,128)(2,1)S(1)} %copy-done.6), kind=kOutput, calls=%fused_computation.23 | convolution fusion | flops 536870912 | bytes 5505024 | tf_op jit(solution)/shard_map/dot_general | solution.py:31
  150.0 2.0 copy-done
  152.0 3.6 %fusion = f32[384,512]{1,0:T(8,128)} fusion(bf16[4096,512]{1,0:T(8,128)(2,1)S(1)} %bitcast.163, s32[384]{0:T(512)S(1)} %eq.126, s32[4096]{0:T(1024)S(1)} %bitcast.199), kind=kOutput, calls=%fused_computation | convolution fusion | flops 1612185600 | bytes 4998656 | tf_op jit(solution)/shard_map/dot_general | solution.py:31
  155.6 3.6 %fusion.2 = f32[384,512]{1,0:T(8,128)} fusion(bf16[4096,512]{1,0:T(8,128)(2,1)S(1)} %bitcast.164, s32[384]{0:T(512)S(1)} %eq.120, s32[4096]{0:T(1024)S(1)} %bitcast.198), kind=kOutput, calls=%fused_computation.2 | convolution fusion | flops 1612185600 | bytes 4998656 | tf_op jit(solution)/shard_map/dot_general | solution.py:31
  159.2 2.7 %fusion.4 = f32[384,512]{1,0:T(8,128)S(1)} fusion(bf16[4096,512]{1,0:T(8,128)(2,1)S(1)} %bitcast.165, s32[384]{0:T(512)S(1)} %eq.114, s32[4096]{0:T(1024)S(1)} %bitcast.197), kind=kOutput, calls=%fused_computation.4 | convolution fusion | flops 1612185600 | bytes 4998656 | tf_op jit(solution)/shard_map/dot_general | solution.py:31
  161.9 2.9 %fusion.8 = f32[384,512]{1,0:T(8,128)S(1)} fusion(bf16[4096,512]{1,0:T(8,128)(2,1)S(1)} %bitcast.166, s32[384]{0:T(512)S(1)} %eq.103, s32[4096]{0:T(1024)S(1)} %bitcast.196), kind=kOutput, calls=%fused_computation.8 | convolution fusion | flops 1612185600 | bytes 4998656 | tf_op jit(solution)/shard_map/dot_general | solution.py:31
  164.8 1.5 fusion.46
  169.5 2.4 collective-permute-start.4
  172.0 2.1 collective-permute-done.4
  175.1 6.8 %all-to-all-start.3 = ((f32[8,224,128]{2,1,0:T(8,128)}), f32[8,224,128]{2,1,0:T(8,128)S(1)}, u32[]{:S(2)}, u32[]{:S(2)}) async-start(f32[8,224,128]{2,1,0:T(8,128)} %fusion.34), calls=%async_computation.3 | async-start | bytes 1835008 | tf_op jit(solution)/shard_map/all_to_all | solution.py:115
  182.0 26.4 %all-to-all-done.3 = f32[8,224,128]{2,1,0:T(8,128)S(1)} async-done(((f32[8,224,128]{2,1,0:T(8,128)}), f32[8,224,128]{2,1,0:T(8,128)S(1)}, u32[]{:S(2)}, u32[]{:S(2)}) %all-to-all-start.3) | async-done | bytes 917536 | tf_op jit(solution)/shard_map/all_to_all | solution.py:115
  209.1 4.9 %all-to-all-start.5 = ((f32[32,3,128]{2,1,0:T(4,128)}), f32[32,3,128]{2,1,0:T(4,128)S(1)}, u32[]{:S(2)}, u32[]{:S(2)}) async-start(f32[32,3,128]{2,1,0:T(4,128)} %copy.231), calls=%async_computation.5 | async-start | bytes 131072 | tf_op jit(solution)/shard_map/all_to_all | solution.py:124
  214.6 8.2 %all-to-all-done.5 = f32[32,3,128]{2,1,0:T(4,128)S(1)} async-done(((f32[32,3,128]{2,1,0:T(4,128)}), f32[32,3,128]{2,1,0:T(4,128)S(1)}, u32[]{:S(2)}, u32[]{:S(2)}) %all-to-all-start.5) | async-done | bytes 49184 | tf_op jit(solution)/shard_map/all_to_all | solution.py:124
  222.8 3.3 %all-to-all-start.4 = ((f32[4,32,128]{2,1,0:T(8,128)}), f32[4,32,128]{2,1,0:T(8,128)S(1)}, u32[]{:S(2)}, u32[]{:S(2)}) async-start(f32[4,32,128]{2,1,0:T(8,128)} %fusion.49), calls=%async_computation.4 | async-start | bytes 131072 | tf_op jit(solution)/shard_map/all_to_all | solution.py:121
  226.2 4.4 %all-to-all-done.4 = f32[4,32,128]{2,1,0:T(8,128)S(1)} async-done(((f32[4,32,128]{2,1,0:T(8,128)}), f32[4,32,128]{2,1,0:T(8,128)S(1)}, u32[]{:S(2)}, u32[]{:S(2)}) %all-to-all-start.4) | async-done | bytes 65568 | tf_op jit(solution)/shard_map/all_to_all | solution.py:121
  230.6 18.7 %all_to_all.36 = f32[8,152,128]{2,1,0:T(8,128)S(1)} all-to-all(f32[8,152,128]{2,1,0:T(8,128)S(1)} %broadcast_in_dim.34), channel_id=1, replica_groups=mesh['y'=8,'core'=2,'x'=4,'z'=8] {'y'}, dimensions={0} | all-to-all | bytes 1245184 | tf_op jit(solution)/shard_map/all_to_all | solution.py:129
  249.4 6.2 %collective-permute-start.5 = (f32[8,152,128]{2,1,0:T(8,128)S(1)}, f32[8,152,128]{2,1,0:T(8,128)S(1)}, u32[]{:S(2)}, u32[]{:S(2)}) collective-permute-start(f32[8,152,128]{2,1,0:T(8,128)S(1)} %all_to_all.36), channel_id=1, source_target_pairs={{0,32},{32,0},{1,33},{33,1},{2,34},{34,2},{3,35},{35,3},{4,36},{36... | collective-permute-start | bytes 1867784 | tf_op jit(solution)/shard_map/ppermute | solution.py:36
  (89 shorter events, 26.4 us)
Async XLA Ops:
  16.3 11.9 %copy-start.4 = (bf16[2,2048,128]{2,1,0:T(8,128)(2,1)S(1)}, bf16[2,2048,128]{2,1,0:T(8,128)(2,1)}, u32[]{:S(2)}) copy-start(bf16[2,2048,128]{2,1,0:T(8,128)(2,1)} %param.9) | copy-start | bytes 3145732
  16.3 17.3 %copy-start.12 = (s32[2,2048,4]{1,2,0:T(4,128)S(1)}, s32[2,2048,4]{1,2,0:T(4,128)}, u32[]{:S(2)}) copy-start(s32[2,2048,4]{1,2,0:T(4,128)} %param.13) | copy-start | bytes 196612
  16.3 108.7 %all-to-all-start.1 = ((bf16[8,512,512]{1,2,0:T(8,128)(2,1)}), bf16[8,512,512]{1,2,0:T(8,128)(2,1)}, u32[]{:S(2)}, u32[]{:S(2)}) async-start(bf16[8,512,512]{1,2,0:T(8,128)(2,1)} %stack.34), calls=%async_computation.1 | async-start | bytes 8388608 | tf_op jit(solution)/shard_map/all_to_all | solution.py:70
  28.1 32.4 %copy-start.8 = (s32[32,4,12]{0,1,2:T(4,128)S(1)}, s32[32,4,12]{0,1,2:T(4,128)}, u32[]{:S(2)}) copy-start(s32[32,4,12]{0,1,2:T(4,128)} %param.14) | copy-start | bytes 18436
  28.2 24.6 %collective-permute-start = (bf16[4096,128]{1,0:T(8,128)(2,1)S(1)}, bf16[4096,128]{1,0:T(8,128)(2,1)S(1)}, u32[]{:S(2)}, u32[]{:S(2)}) collective-permute-start(bf16[4096,128]{1,0:T(8,128)(2,1)S(1)} %bitcast.177), channel_id=1, source_target_pairs={{0,24},{8,0},{16,8},{24,16},{1,25},{9,1},{17,9},{25,17},{2,26},{10... | collective-permute-start | bytes 3145736 | tf_op jit(solution)/shard_map/ppermute | solution.py:36
  31.0 26.7 %collective-permute-start.1 = (bf16[4096,128]{1,0:T(8,128)(2,1)S(1)}, bf16[4096,128]{1,0:T(8,128)(2,1)S(1)}, u32[]{:S(2)}, u32[]{:S(2)}) collective-permute-start(bf16[4096,128]{1,0:T(8,128)(2,1)S(1)} %bitcast.178), channel_id=1, source_target_pairs={{0,8},{8,16},{16,24},{24,0},{1,9},{9,17},{17,25},{25,1},{2,10},{10... | collective-permute-start | bytes 3145736 | tf_op jit(solution)/shard_map/ppermute | solution.py:36
  53.7 18.6 %collective-permute-start.3 = (bf16[2048,128]{1,0:T(8,128)(2,1)}, bf16[2048,128]{1,0:T(8,128)(2,1)}, u32[]{:S(2)}, u32[]{:S(2)}) collective-permute-start(bf16[2048,128]{1,0:T(8,128)(2,1)} %slice.91), channel_id=1, source_target_pairs={{0,24},{8,0},{16,8},{24,16},{1,25},{9,1},{17,9},{25,17},{2,26},{10... | collective-permute-start | bytes 1572872 | tf_op jit(solution)/shard_map/ppermute | solution.py:36
  58.6 13.8 %collective-permute-start.2 = (bf16[2048,128]{1,0:T(8,128)(2,1)}, bf16[2048,128]{1,0:T(8,128)(2,1)}, u32[]{:S(2)}, u32[]{:S(2)}) collective-permute-start(bf16[2048,128]{1,0:T(8,128)(2,1)} %slice.90), channel_id=1, source_target_pairs={{0,8},{8,16},{16,24},{24,0},{1,9},{9,17},{17,25},{25,1},{2,10},{10... | collective-permute-start | bytes 1572872 | tf_op jit(solution)/shard_map/ppermute | solution.py:36
  124.9 39.8 %all-to-all-start.2 = ((bf16[4,128,512]{1,2,0:T(8,128)(2,1)}), bf16[4,128,512]{1,2,0:T(8,128)(2,1)S(1)}, u32[]{:S(2)}, u32[]{:S(2)}) async-start(bf16[4,128,512]{1,2,0:T(8,128)(2,1)} %bitcast.36), calls=%async_computation.2 | async-start | bytes 1048576 | tf_op jit(solution)/shard_map/all_to_all | solution.py:75
  134.9 6.5 %copy-start.6 = (bf16[128,4096]{1,0:T(8,128)(2,1)S(1)}, bf16[128,4096]{1,0:T(8,128)(2,1)}, u32[]{:S(2)}) copy-start(bf16[128,4096]{1,0:T(8,128)(2,1)} %copy.217) | copy-start | bytes 3145732
  141.4 3.8 %copy-start.1 = (bf16[512,4096]{1,0:T(8,128)(2,1)S(1)}, bf16[512,4096]{1,0:T(8,128)(2,1)}, u32[]{:S(2)}) copy-start(bf16[512,4096]{1,0:T(8,128)(2,1)} %copy.214) | copy-start | bytes 12582916
  141.5 3.9 %copy-start.7 = (bf16[128,4096]{1,0:T(8,128)(2,1)S(1)}, bf16[128,4096]{1,0:T(8,128)(2,1)}, u32[]{:S(2)}) copy-start(bf16[128,4096]{1,0:T(8,128)(2,1)} %copy.216) | copy-start | bytes 3145732
  146.8 1.5 copy-start.5
  149.8 2.2 copy-start
  164.8 3.5 %copy-start.3 = (f32[384,512]{1,0:T(8,128)S(1)}, f32[384,512]{1,0:T(8,128)}, u32[]{:S(2)}) copy-start(f32[384,512]{1,0:T(8,128)} %fusion) | copy-start | bytes 2359300
  164.8 3.7 %copy-start.2 = (f32[384,512]{1,0:T(8,128)S(1)}, f32[384,512]{1,0:T(8,128)}, u32[]{:S(2)}) copy-start(f32[384,512]{1,0:T(8,128)} %fusion.2) | copy-start | bytes 2359300
  169.5 4.5 %collective-permute-start.4 = (f32[8,224,128]{2,1,0:T(8,128)S(1)}, f32[8,224,128]{2,1,0:T(8,128)S(1)}, u32[]{:S(2)}, u32[]{:S(2)}) collective-permute-start(f32[8,224,128]{2,1,0:T(8,128)S(1)} %select_bitcast_fusion), channel_id=1, source_target_pairs={{0,32},{32,0},{1,33},{33,1},{2,34},{34,2},{3,35},{35,3},{4,36},{36... | collective-permute-start | bytes 2752520 | tf_op jit(solution)/shard_map/ppermute | solution.py:36
  175.1 33.2 %all-to-all-start.3 = ((f32[8,224,128]{2,1,0:T(8,128)}), f32[8,224,128]{2,1,0:T(8,128)S(1)}, u32[]{:S(2)}, u32[]{:S(2)}) async-start(f32[8,224,128]{2,1,0:T(8,128)} %fusion.34), calls=%async_computation.3 | async-start | bytes 1835008 | tf_op jit(solution)/shard_map/all_to_all | solution.py:115
  209.1 13.7 %all-to-all-start.5 = ((f32[32,3,128]{2,1,0:T(4,128)}), f32[32,3,128]{2,1,0:T(4,128)S(1)}, u32[]{:S(2)}, u32[]{:S(2)}) async-start(f32[32,3,128]{2,1,0:T(4,128)} %copy.231), calls=%async_computation.5 | async-start | bytes 131072 | tf_op jit(solution)/shard_map/all_to_all | solution.py:124
  222.8 7.7 %all-to-all-start.4 = ((f32[4,32,128]{2,1,0:T(8,128)}), f32[4,32,128]{2,1,0:T(8,128)S(1)}, u32[]{:S(2)}, u32[]{:S(2)}) async-start(f32[4,32,128]{2,1,0:T(8,128)} %fusion.49), calls=%async_computation.4 | async-start | bytes 131072 | tf_op jit(solution)/shard_map/all_to_all | solution.py:121
  249.4 9.2 %copy-start.9 = (f32[1,4,12,1024]{3,1,2,0:T(4,128)S(1)}, f32[1,4,12,1024]{3,1,2,0:T(4,128)}, u32[]{:S(2)}) copy-start(f32[1,4,12,1024]{3,1,2,0:T(4,128)} %param.17) | copy-start | bytes 589828
  249.4 9.2 %copy-start.10 = (f32[1,4,12,1024]{3,1,2,0:T(4,128)S(1)}, f32[1,4,12,1024]{3,1,2,0:T(4,128)}, u32[]{:S(2)}) copy-start(f32[1,4,12,1024]{3,1,2,0:T(4,128)} %param.16) | copy-start | bytes 589828
  249.4 9.2 %copy-start.11 = (f32[1,4,12,1024]{3,1,2,0:T(4,128)S(1)}, f32[1,4,12,1024]{3,1,2,0:T(4,128)}, u32[]{:S(2)}) copy-start(f32[1,4,12,1024]{3,1,2,0:T(4,128)} %param.15) | copy-start | bytes 589828
  249.4 7.9 %collective-permute-start.5 = (f32[8,152,128]{2,1,0:T(8,128)S(1)}, f32[8,152,128]{2,1,0:T(8,128)S(1)}, u32[]{:S(2)}, u32[]{:S(2)}) collective-permute-start(f32[8,152,128]{2,1,0:T(8,128)S(1)} %all_to_all.36), channel_id=1, source_target_pairs={{0,32},{32,0},{1,33},{33,1},{2,34},{34,2},{3,35},{35,3},{4,36},{36... | collective-permute-start | bytes 1867784 | tf_op jit(solution)/shard_map/ppermute | solution.py:36
